TPU v7x, 32 devices: a whole 2x2x4 slice. The times are simulated.
32 devices in a mesh: groups: 2 (over x), dp: 16 (over z, y, core).
Axes of the slice: x: 2, y: 2, z: 4, core: 2. Of those that a mesh axis runs over, the one named last changes fastest.
Arguments:
- states: bfloat16 [16384, 1024], P(('groups', 'dp')), parts along dimension 0, may hold values from -6 to 6
- lengths: int32 [64], P(('groups', 'dp')), parts along dimension 0, may hold values from 1 to 256, as said below
- norm_gain: bfloat16 [1024], replicated, may hold values from 0.5 to 2
- w_gate: bfloat16 [1024, 1536], replicated, may hold values from -0.1875 to 0.1875
- w_up: bfloat16 [1024, 1536], replicated, may hold values from -0.1875 to 0.1875
- w_down: bfloat16 [1536, 1024], replicated, may hold values from -0.15625 to 0.15625
- context: bfloat16 [64, 4096], P('groups', 'dp'), parts along dimension 0, may hold values from -6 to 6
- w_out: bfloat16 [4096, 4096], P('dp'), may hold values from -0.09375 to 0.09375
- resid_stream: bfloat16 [64, 4096], P('groups'), parts along dimension 0, may hold values from -6 to 6
- teacher_gain: bfloat16 [4096], replicated, may hold values from 0.5 to 2
Outputs:
- gram_loss: float32 [2], P('groups'), parts along dimension 0
- grad_gate: float32 [2048, 1536], P(('groups', 'dp')), parts along dimension 0
- grad_up: float32 [2048, 1536], P(('groups', 'dp')), parts along dimension 0
- grad_down: float32 [3072, 1024], P(('groups', 'dp')), parts along dimension 0
There are 2 independent parts, one for each index of `groups`. A program takes and returns all parts, laid end to end along the dimension named above; an argument that names none is the same for every part. Nothing has to cross between parts.
Inputs may be any that keep to these rules, and one draw needn't show every extreme that they name: `lengths`: some document of every group fills all 256 slots and some has a single valid token.
All inputs are finite; a program needn't handle non-finite values.
Results may differ from a plain program's by a relative error of at most 0.004.
Values may be sent and summed in bfloat16 or wider, within the bound.
A program may use at most 128 MiB of HBM per device.

v0:
```python
import jax
import jax.numpy as jnp
from jax import lax
from jax.sharding import PartitionSpec as P

EPS = 1e-06
LOSS_SCALE = 4096.0


def teacher_embed(attn_rows, resid_rows, teacher_gain):
    scaled_rows = teacher_gain.astype(jnp.float32) * (resid_rows.astype(jnp.float32) + attn_rows)
    inv_teacher = lax.rsqrt(jnp.sum(scaled_rows * scaled_rows, axis=1, keepdims=True) + EPS)
    return (scaled_rows * inv_teacher).astype(jnp.bfloat16)


def rows_product(left_rows, right_rows):
    return lax.dot_general(
        left_rows, right_rows, (((1,), (1,)), ((), ())), preferred_element_type=jnp.float32
    )


def cols_product(left_cols, right_cols):
    return lax.dot_general(
        left_cols, right_cols, (((0,), (0,)), ((), ())), preferred_element_type=jnp.float32
    )


def per_device(
    states, lengths, norm_gain, w_gate, w_up, w_down, context, w_out, resid_stream, teacher_gain
):
    dp = lax.axis_size("dp")
    my_index = lax.axis_index("dp")
    doc_dev = lengths.shape[0]
    seq_len = states.shape[0] // doc_dev
    model_width = states.shape[1]
    hidden_width = w_gate.shape[1]
    feat = w_out.shape[1] // dp
    high = lax.Precision.HIGHEST
    partial_attn = jnp.dot(context, w_out, preferred_element_type=jnp.float32)
    attn_cols = lax.psum_scatter(partial_attn, "dp", scatter_dimension=1, tiled=True)
    resid_cols = lax.dynamic_slice_in_dim(resid_stream, my_index * feat, feat, 1)
    gain_cols = lax.dynamic_slice_in_dim(teacher_gain, my_index * feat, feat, 0)
    scaled = gain_cols.astype(jnp.float32) * (resid_cols.astype(jnp.float32) + attn_cols)
    gram_part = lax.dot_general(scaled, scaled, (((1,), (1,)), ((), ())), precision=high)
    states_wide = states.astype(jnp.float32)
    inv_rms = lax.rsqrt(jnp.mean(states_wide * states_wide, axis=1, keepdims=True) + EPS)
    normed = (states_wide * inv_rms * norm_gain.astype(jnp.float32)).astype(jnp.bfloat16)
    gate_pre = jnp.dot(normed, w_gate, preferred_element_type=jnp.float32)
    up_pre = jnp.dot(normed, w_up, preferred_element_type=jnp.float32)
    hidden = (jax.nn.silu(gate_pre) * up_pre).astype(jnp.bfloat16)
    positions = lax.broadcasted_iota(jnp.int32, (doc_dev, seq_len), 1)
    valid_mask = (positions < lengths[:, None]).astype(jnp.float32)
    counts = lengths.astype(jnp.float32)
    hidden_sum = jnp.sum(
        hidden.astype(jnp.float32).reshape(doc_dev, seq_len, hidden_width) * valid_mask[:, :, None],
        axis=1,
    )
    state_sum = jnp.sum(
        states_wide.reshape(doc_dev, seq_len, model_width) * valid_mask[:, :, None], axis=1
    )
    packed = jnp.concatenate(
        [hidden_sum, state_sum, jnp.broadcast_to(counts[:, None], (doc_dev, 128))], axis=1
    )
    packed_all = lax.all_gather(packed, "dp", axis=0, tiled=True)
    hidden_all = packed_all[:, :hidden_width]
    state_all = packed_all[:, hidden_width : hidden_width + model_width]
    count_all = packed_all[:, hidden_width + model_width :][:, :1]
    gram_raw = lax.psum(gram_part, "dp")
    docs = gram_raw.shape[0]
    eye = jnp.eye(docs, dtype=jnp.float32)
    inv_col = lax.rsqrt(jnp.sum(gram_raw * eye, axis=1, keepdims=True) + EPS)
    inv_row = lax.rsqrt(jnp.sum(gram_raw * eye, axis=0, keepdims=True) + EPS)
    gram_teacher = gram_raw * inv_col * inv_row
    pooled = (
        state_all + jnp.dot(hidden_all, w_down.astype(jnp.float32), precision=high)
    ) / count_all
    inv_norm = lax.rsqrt(jnp.sum(pooled * pooled, axis=1, keepdims=True) + EPS)
    unit_rows = pooled * inv_norm
    embed = unit_rows.astype(jnp.bfloat16)
    gram_diff = rows_product(embed, embed) - gram_teacher
    diff_norm = jnp.sqrt(jnp.sum(gram_diff * gram_diff) + EPS)
    teacher_norm = jnp.sqrt(jnp.sum(gram_teacher * gram_teacher))
    gram_loss = (diff_norm / teacher_norm).reshape(1)
    d_gram = LOSS_SCALE * gram_diff / (diff_norm * teacher_norm)
    d_embed = 2.0 * jnp.dot(d_gram, embed.astype(jnp.float32), precision=high)
    along = jnp.sum(unit_rows * d_embed, axis=1, keepdims=True)
    d_pooled = (d_embed - unit_rows * along) * inv_norm
    d_all = (d_pooled / count_all).astype(jnp.bfloat16)
    down_rows = hidden_width // dp
    own_hidden = lax.dynamic_slice_in_dim(hidden_all, my_index * down_rows, down_rows, 1)
    grad_down = lax.dot_general(
        own_hidden, d_all.astype(jnp.float32), (((0,), (0,)), ((), ())), precision=high
    )
    d_doc = lax.dynamic_slice_in_dim(d_all, my_index * doc_dev, doc_dev, 0)
    d_hidden = rows_product(d_doc, w_down)
    d_hidden_tok = (d_hidden[:, None, :] * valid_mask[:, :, None]).reshape(
        doc_dev * seq_len, hidden_width
    )
    sigmoid_gate = jax.nn.sigmoid(gate_pre)
    d_gate = (
        d_hidden_tok * up_pre * sigmoid_gate * (1.0 + gate_pre * (1.0 - sigmoid_gate))
    ).astype(jnp.bfloat16)
    d_up = (d_hidden_tok * jax.nn.silu(gate_pre)).astype(jnp.bfloat16)
    rows = model_width // dp
    terms = jnp.concatenate([cols_product(normed, d_gate), cols_product(normed, d_up)], axis=1)
    terms = terms.astype(jnp.bfloat16)
    swapped = lax.all_to_all(terms.reshape(dp, rows, 2 * hidden_width), "dp", 0, 0)
    total = jnp.sum(swapped.astype(jnp.float32), axis=0)
    return (gram_loss, total[:, :hidden_width], total[:, hidden_width:], grad_down)


def solution(mesh):
    in_specs = (
        P(("groups", "dp"), None),
        P(("groups", "dp")),
        P(),
        P(),
        P(),
        P(),
        P("groups", "dp"),
        P("dp", None),
        P("groups", None),
        P(),
    )
    out_specs = (
        P("groups"),
        P(("groups", "dp"), None),
        P(("groups", "dp"), None),
        P(("groups", "dp"), None),
    )
    return jax.shard_map(
        per_device, mesh=mesh, in_specs=in_specs, out_specs=out_specs, check_vma=False
    )
```

profile of v0, /device:TPU:13, one launch (start us, length us, event | category | flops | bytes accessed | tf_op | source)
XLA Modules:
  0.0 300.5 jit_solution(8370609172329494020)
XLA Ops:
  7.2 0.0 reduce-scatter.2.cloned.1.call-start
  7.2 3.0 %fusion.35 = f32[32,4096]{1,0:T(8,128)} fusion(bf16[32,256]{1,0:T(8,128)(2,1)} %param.16, bf16[256,4096]{1,0:T(8,128)(2,1)} %param.17), kind=kOutput, calls=%fused_computation.65 | convolution fusion | flops 67108864 | bytes 2637824 | tf_op jit(solution)/shard_map/dot_general | solution.py:39
  10.3 0.0 reduce-scatter.2.cloned.1.call-update
  10.3 0.1 fusion.30
  10.4 1.5 multiply_reduce_fusion.1
  11.9 1.5 multiply_reduce_fusion
  13.5 4.2 %fusion.33 = f32[512,1536]{1,0:T(8,128)S(1)} fusion(bf16[1024,1536]{1,0:T(8,128)(2,1)} %param.13, f32[1024]{0:T(1024)S(1)} %convert_element_type.57, f32[512]{0:T(512)S(1)} %add_rsqrt_fusion, bf16[512,1024]{1,0:T(8,128)(2,1)} %param.10), kind=kOutput, calls=%fused_computation.63 | convolution fusion | flops 1612709888 | bytes 7346176 | tf_op jit(solution)/shard_map/dot_general | solution.py:48
  17.7 3.9 %fusion = (f32[2,1536]{1,0:T(2,128)S(1)}, f32[512,1536]{1,0:T(8,128)}) fusion(f32[2,256]{1,0:T(2,128)S(1)} %get-tuple-element.11, f32[512,1536]{1,0:T(8,128)S(1)} %fusion.33, bf16[1024,1536]{1,0:T(8,128)(2,1)S(1)} %copy-done, f32[1024]{0:T(1024)S(1)} %convert_element_type.57, f32[512]{0:T(512)S(1)} %add_rsqrt_fusion, bf16[512,1024]{1,0:T(8,128)(2,1)S(1)} %copy-done.3), kind=kOutput, calls=%fused_computation.5 | convolution fusion | flops 1619784704 | bytes 10506240 | tf_op jit(solution)/shard_map/dot_general | solution.py:49
  21.6 0.1 broadcast_in_dim.2
  21.6 18.0 %all-gather = f32[16,2,2688]{2,1,0:T(2,128)} all-gather(f32[1,2,2688]{2,1,0:T(2,128)S(1)} %maximum_bitcast_fusion), channel_id=1, replica_groups=mesh['groups'=2,'dp'=16] {'dp'}, dimensions={0}, use_global_device_ids=true | all-gather | bytes 365568 | tf_op jit(solution)/shard_map/all_gather | solution.py:64
  39.6 1.2 reshape.93
  40.9 0.8 dynamic-slice_convert_fusion
  41.7 0.1 slice_reduce_fusion
  41.8 3.7 %multiply_reduce_fusion.3 = (f32[32]{0:T(128)S(1)}, f32[32,1024]{1,0:T(8,128)S(1)}) fusion(f32[32]{0:T(128)S(1)} %slice_reduce_fusion, bf16[1536,1024]{1,0:T(8,128)(2,1)} %param.15, f32[32,2688]{1,0:T(8,128)} %copy-done.5), kind=kOutput, calls=%fused_computation.25 | convolution fusion | flops 604110848 | bytes 3604736 | tf_op jit(solution)/shard_map/dot_general | solution.py:75
  45.5 20.7 %reduce-scatter.2.cloned.1.call-done = f32[32,256]{1,0:T(8,128)} async-done(((f32[32,4096]{1,0:T(8,128)}), f32[32,256]{1,0:T(8,128)}) %reduce-scatter.2.cloned.1.call-update) | async-done | bytes 32784 | tf_op jit(solution)/shard_map/reduce_scatter | solution.py:40
  66.2 1.0 fusion.9
  67.2 45.7 %psum.7 = f32[32,32]{1,0:T(8,128)S(1)} all-reduce(f32[32,32]{1,0:T(8,128)S(1)} %fusion.9), channel_id=1, replica_groups=mesh['groups'=2,'dp'=16] {'dp'}, use_global_device_ids=true, to_apply=%region_5.6 | all-reduce | flops 1024 | bytes 8192 | tf_op jit(solution)/shard_map/psum | solution.py:68
  112.9 0.1 fusion.21
  113.1 0.7 multiply_reduce_fusion.4
  114.4 0.8 multiply_reduce_fusion.5
  116.0 0.4 multiply_reduce_fusion.2
  116.3 0.1 divide_convert_fusion
  116.4 3.0 %fusion.24 = f32[2,1536]{1,0:T(2,128)S(1)} fusion(bf16[1536,1024]{1,0:T(8,128)(2,1)} %param.15, bf16[32,1024]{1,0:T(8,128)(2,1)S(1)} %divide_convert_fusion, s32[]{:T(128)S(6)} %select_n.11), kind=kOutput, calls=%fused_computation.48 | convolution fusion | flops 6291456 | bytes 3162116 | tf_op jit(solution)/shard_map/dot_general | solution.py:17
  119.5 3.5 %fusion.5 = (bf16[512,1536]{1,0:T(8,128)(2,1)S(1)}, bf16[512,1536]{1,0:T(8,128)(2,1)S(1)}) fusion(f32[512,1536]{1,0:T(8,128)} %get-tuple-element.13, f32[512,1536]{1,0:T(8,128)S(1)} %copy-done.2, f32[512]{0:T(512)S(1)} %bitcast.38, f32[2,1536]{1,0:T(2,128)S(1)} %fusion.24), kind=kLoop, calls=%fused_computation.11 | loop fusion | flops 11010048 | bytes 9451520 | tf_op jit(solution)/shard_map/convert_element_type | solution.py:102
  123.0 1.9 convolution_convert_fusion.1
  125.0 1.9 convolution_convert_fusion
  126.9 3.5 %pad_maximum_fusion = bf16[16,64,3072]{2,1,0:T(8,128)(2,1)} fusion(bf16[16,64,1536]{2,1,0:T(8,128)(2,1)S(1)} %bitcast.37, bf16[16,64,1536]{2,1,0:T(8,128)(2,1)S(1)} %bitcast.36), kind=kLoop, calls=%fused_computation.1 | loop fusion | flops 12582912 | bytes 12582912 | tf_op jit(solution)/shard_map/concatenate | solution.py:105
  130.4 19.8 %all-to-all-start = ((bf16[16,64,3072]{2,1,0:T(8,128)(2,1)}), bf16[16,64,3072]{2,1,0:T(8,128)(2,1)}, u32[]{:S(2)}, u32[]{:S(2)}) async-start(bf16[16,64,3072]{2,1,0:T(8,128)(2,1)} %pad_maximum_fusion), calls=%async_computation.1 | async-start | bytes 12582912 | tf_op jit(solution)/shard_map/all_to_all | solution.py:107
  150.2 1.2 fusion.13
  151.4 136.2 %all-to-all-done = bf16[16,64,3072]{2,1,0:T(8,128)(2,1)} async-done(((bf16[16,64,3072]{2,1,0:T(8,128)(2,1)}), bf16[16,64,3072]{2,1,0:T(8,128)(2,1)}, u32[]{:S(2)}, u32[]{:S(2)}) %all-to-all-start) | async-done | bytes 6291488 | tf_op jit(solution)/shard_map/all_to_all | solution.py:107
  287.6 4.0 %convert_reduce_fusion = f32[64,3072]{1,0:T(8,128)S(1)} fusion(bf16[16,64,3072]{2,1,0:T(8,128)(2,1)} %all-to-all-done), kind=kLoop, calls=%fused_computation | loop fusion | flops 6094848 | bytes 7077888 | tf_op jit(solution)/shard_map/reduce_sum | solution.py:108
  291.6 0.9 fusion.34
  (25 shorter events, 0.1 us)
Async XLA Ops:
  7.2 10.5 %copy-start = (bf16[1024,1536]{1,0:T(8,128)(2,1)S(1)}, bf16[1024,1536]{1,0:T(8,128)(2,1)}, u32[]{:S(2)}) copy-start(bf16[1024,1536]{1,0:T(8,128)(2,1)} %param.14) | copy-start | bytes 9437188
  7.2 3.1 %copy-start.7 = (s32[2]{0:T(128)S(1)}, s32[2]{0:T(128)}, u32[]{:S(2)}) copy-start(s32[2]{0:T(128)} %param.11) | copy-start | bytes 28
  7.2 4.7 %copy-start.6 = (bf16[1024]{0:T(1024)(128)(2,1)S(1)}, bf16[1024]{0:T(1024)(128)(2,1)}, u32[]{:S(2)}) copy-start(bf16[1024]{0:T(1024)(128)(2,1)} %param.12) | copy-start | bytes 6148
  7.2 59.0 %reduce-scatter.2.cloned.1.call-start = ((), (), s32[]{:S(2)}) async-start(), calls=%async_computation.2 | async-start | bytes 557056 | tf_op jit(solution)/shard_map/reduce_scatter | solution.py:40
  13.5 4.2 %copy-start.3 = (bf16[512,1024]{1,0:T(8,128)(2,1)S(1)}, bf16[512,1024]{1,0:T(8,128)(2,1)}, u32[]{:S(2)}) copy-start(bf16[512,1024]{1,0:T(8,128)(2,1)} %param.10) | copy-start | bytes 3145732
  17.7 3.9 %copy-start.1 = (f32[512,1536]{1,0:T(8,128)}, f32[512,1536]{1,0:T(8,128)S(1)}, u32[]{:S(2)}) copy-start(f32[512,1536]{1,0:T(8,128)S(1)} %fusion.33) | copy-start | bytes 9437188
  40.9 0.8 copy-start.5
  116.0 3.5 %copy-start.2 = (f32[512,1536]{1,0:T(8,128)S(1)}, f32[512,1536]{1,0:T(8,128)}, u32[]{:S(2)}) copy-start(f32[512,1536]{1,0:T(8,128)} %copy-done.1) | copy-start | bytes 9437188
  119.5 3.5 %copy-start.4 = (bf16[512,1024]{1,0:T(8,128)(2,1)S(1)}, bf16[512,1024]{1,0:T(8,128)(2,1)}, u32[]{:S(2)}) copy-start(bf16[512,1024]{1,0:T(8,128)(2,1)} %param.10) | copy-start | bytes 3145732
  130.4 19.8 %slice-start = ((f32[32,2688]{1,0:T(8,128)}), f32[32,1536]{1,0:T(8,128)S(1)}, s32[]{:S(2)}) async-start(f32[32,2688]{1,0:T(8,128)} %copy-done.5), calls=%async_computation.3 | async-start | bytes 393216 | tf_op jit(solution)/shard_map/slice | solution.py:65
  130.4 157.2 %all-to-all-start = ((bf16[16,64,3072]{2,1,0:T(8,128)(2,1)}), bf16[16,64,3072]{2,1,0:T(8,128)(2,1)}, u32[]{:S(2)}, u32[]{:S(2)}) async-start(bf16[16,64,3072]{2,1,0:T(8,128)(2,1)} %pad_maximum_fusion), calls=%async_computation.1 | async-start | bytes 12582912 | tf_op jit(solution)/shard_map/all_to_all | solution.py:107
Sparse Core Ops, SparseCore 0:
  11.6 54.5 reduce-scatter.1
where the time goes:
time: 301 us
  waiting for transfers between devices  157 us (52%)
  blocking collectives  63.7 us (21%)
  matrix products  25.1 us (8%)
  starting transfers between devices  19.8 us (7%)
  between operations  16.8 us (6%)
  other arithmetic  15.9 us (5%)
    all_to_all x1, waiting for transfers between devices, per_device(): lax.all_to_all(terms.reshape(dp, rows, 2 * hidden_width), 'dp', 0, 0)  136 us
    psum x1, blocking collectives, per_device(): gram_raw = lax.psum(gram_part, 'dp')  45.7 us
    reduce_scatter x1, waiting for transfers between devices, per_device(): lax.psum_scatter(partial_attn, 'dp', scatter_dimension=1, tiled=True)  20.7 us
    all_to_all x1, starting transfers between devices, per_device(): lax.all_to_all(terms.reshape(dp, rows, 2 * hidden_width), 'dp', 0, 0)  19.8 us
    all_gather x1, blocking collectives, per_device(): packed_all = lax.all_gather(packed, 'dp', axis=0, tiled=True)  18 us
  transfers between devices with their start and end apart: 2, of which 2 were waited for; matrix products, arithmetic and copies ran while one was open for 6% of the time, Pallas kernels for 0%

commit v1 on v0

--- a/solution.py
+++ b/solution.py
@@ -65,7 +65,7 @@
     hidden_all = packed_all[:, :hidden_width]
     state_all = packed_all[:, hidden_width : hidden_width + model_width]
     count_all = packed_all[:, hidden_width + model_width :][:, :1]
-    gram_raw = lax.psum(gram_part, "dp")
+    gram_raw = jnp.sum(lax.all_gather(gram_part, "dp"), axis=0)
     docs = gram_raw.shape[0]
     eye = jnp.eye(docs, dtype=jnp.float32)
     inv_col = lax.rsqrt(jnp.sum(gram_raw * eye, axis=1, keepdims=True) + EPS)

time: 301 us -> 266 us (0.88)
  blocking collectives: 63.7 us -> 36.6 us
  starting transfers between devices: 19.8 us -> 9.43 us
    psum x1 -> x0, blocking collectives: 45.7 us -> none  [per_device(): gram_raw = lax.psum(gram_part, 'dp')]
    all_gather x0 -> x1, blocking collectives: none -> 18.7 us  [per_device(): gram_raw = jnp.sum(lax.all_gather(gram_part, 'dp'), axis=0)]
    all_to_all x1, starting transfers between devices: 19.8 us -> 9.39 us  [per_device(): lax.all_to_all(terms.reshape(dp, rows, 2 * hidden_width), 'dp', 0, 0)]
  transfers between devices with their start and end apart: 2 -> 2, of which waited for: 2 -> 2; matrix products, arithmetic and copies ran while one was open for 6% -> 7% of each run, Pallas kernels for 0% -> 0%
where the time goes in v1:
time: 266 us; the launch traced here: 265 us
  waiting for transfers between devices  155 us (58%)
  blocking collectives  36.6 us (14%)
  matrix products  26.4 us (10%)
  other arithmetic  17.1 us (6%)
  between operations  16.7 us (6%)
  starting transfers between devices  9.43 us (4%)
  local copies, waits for them, and re-layouts  3.58 us (1%)
    all_to_all x1, waiting for transfers between devices, per_device(): lax.all_to_all(terms.reshape(dp, rows, 2 * hidden_width), 'dp', 0, 0)  136 us
    reduce_scatter x1, waiting for transfers between devices, per_device(): lax.psum_scatter(partial_attn, 'dp', scatter_dimension=1, tiled=True)  19 us
    all_gather x1, blocking collectives, per_device(): gram_raw = jnp.sum(lax.all_gather(gram_part, 'dp'), axis=0)  18.7 us
    all_gather x1, blocking collectives, per_device(): packed_all = lax.all_gather(packed, 'dp', axis=0, tiled=True)  18 us
    all_to_all x1, starting transfers between devices, per_device(): lax.all_to_all(terms.reshape(dp, rows, 2 * hidden_width), 'dp', 0, 0)  9.39 us
  transfers between devices with their start and end apart: 2, of which 2 were waited for; matrix products, arithmetic and copies ran while one was open for 7% of the time, Pallas kernels for 0%

profile of v1, /device:TPU:13, one launch (start us, length us, event | category | flops | bytes accessed | tf_op | source)
XLA Modules:
  0.0 265.0 jit_solution(11175572083951547409)
XLA Ops:
  7.2 3.0 %fusion.35 = f32[32,4096]{1,0:T(8,128)} fusion(bf16[32,256]{1,0:T(8,128)(2,1)} %param.16, bf16[256,4096]{1,0:T(8,128)(2,1)} %param.17), kind=kOutput, calls=%fused_computation.65 | convolution fusion | flops 67108864 | bytes 2637824 | tf_op jit(solution)/shard_map/dot_general | solution.py:39
  10.3 0.1 fusion.30
  10.4 1.5 multiply_reduce_fusion.1
  12.0 1.5 multiply_reduce_fusion
  13.5 4.2 %fusion.33 = f32[512,1536]{1,0:T(8,128)S(1)} fusion(bf16[1024,1536]{1,0:T(8,128)(2,1)} %param.13, f32[1024]{0:T(1024)S(1)} %convert_element_type.57, f32[512]{0:T(512)S(1)} %add_rsqrt_fusion, bf16[512,1024]{1,0:T(8,128)(2,1)} %param.10), kind=kOutput, calls=%fused_computation.63 | convolution fusion | flops 1612709888 | bytes 7346176 | tf_op jit(solution)/shard_map/dot_general | solution.py:48
  17.7 3.9 %fusion = (f32[2,1536]{1,0:T(2,128)S(1)}, f32[512,1536]{1,0:T(8,128)}) fusion(f32[2,256]{1,0:T(2,128)S(1)} %get-tuple-element.11, f32[512,1536]{1,0:T(8,128)S(1)} %fusion.33, bf16[1024,1536]{1,0:T(8,128)(2,1)S(1)} %copy-done, f32[1024]{0:T(1024)S(1)} %convert_element_type.57, f32[512]{0:T(512)S(1)} %add_rsqrt_fusion, bf16[512,1024]{1,0:T(8,128)(2,1)S(1)} %copy-done.3), kind=kOutput, calls=%fused_computation.5 | convolution fusion | flops 1619784704 | bytes 10506240 | tf_op jit(solution)/shard_map/dot_general | solution.py:49
  21.7 18.0 %all-gather.1 = f32[16,2,2688]{2,1,0:T(2,128)} all-gather(f32[1,2,2688]{2,1,0:T(2,128)S(1)} %maximum_bitcast_fusion), channel_id=1, replica_groups=mesh['groups'=2,'dp'=16] {'dp'}, dimensions={0}, use_global_device_ids=true | all-gather | bytes 365568 | tf_op jit(solution)/shard_map/all_gather | solution.py:64
  39.7 0.6 copy.14
  40.2 1.2 reshape.94
  41.5 0.8 dynamic-slice_convert_fusion
  42.3 0.1 slice_reduce_fusion
  42.4 0.6 copy-done.11
  43.0 3.7 %multiply_reduce_fusion.3 = (f32[32]{0:T(128)S(1)}, f32[32,1024]{1,0:T(8,128)S(1)}) fusion(f32[32]{0:T(128)S(1)} %slice_reduce_fusion, bf16[1536,1024]{1,0:T(8,128)(2,1)} %param.15, f32[32,2688]{1,0:T(8,128)} %copy-done.5), kind=kOutput, calls=%fused_computation.25 | convolution fusion | flops 604110848 | bytes 3604736 | tf_op jit(solution)/shard_map/dot_general | solution.py:75
  46.7 0.5 add_rsqrt_fusion.3
  47.2 19.0 %reduce-scatter.2.cloned.1.call-done = f32[32,256]{1,0:T(8,128)} async-done(((f32[32,4096]{1,0:T(8,128)}), f32[32,256]{1,0:T(8,128)}) %reduce-scatter.2.cloned.1.call-update) | async-done | bytes 32784 | tf_op jit(solution)/shard_map/reduce_scatter | solution.py:40
  66.2 1.0 fusion.9
  67.2 18.7 %all-gather = f32[512,32]{1,0:T(8,128)S(1)} all-gather(f32[32,32]{1,0:T(8,128)S(1)} %fusion.9), channel_id=2, replica_groups=mesh['groups'=2,'dp'=16] {'dp'}, dimensions={0}, use_global_device_ids=true | all-gather | bytes 69632 | tf_op jit(solution)/shard_map/all_gather | solution.py:68
  85.9 0.1 fusion.21
  86.1 0.7 multiply_reduce_fusion.4
  87.3 1.6 multiply_reduce_fusion.5
  89.5 1.2 multiply_reduce_fusion.2
  90.7 0.8 divide_convert_fusion
  91.5 2.8 %fusion.24 = f32[2,1536]{1,0:T(2,128)S(1)} fusion(bf16[1536,1024]{1,0:T(8,128)(2,1)} %param.15, bf16[32,1024]{1,0:T(8,128)(2,1)S(1)} %divide_convert_fusion, s32[]{:T(128)S(6)} %select_n.11), kind=kOutput, calls=%fused_computation.48 | convolution fusion | flops 6291456 | bytes 3162116 | tf_op jit(solution)/shard_map/dot_general | solution.py:17
  94.4 3.5 %fusion.5 = (bf16[512,1536]{1,0:T(8,128)(2,1)S(1)}, bf16[512,1536]{1,0:T(8,128)(2,1)S(1)}) fusion(f32[512,1536]{1,0:T(8,128)} %get-tuple-element.13, f32[512,1536]{1,0:T(8,128)S(1)} %copy-done.2, f32[512]{0:T(512)S(1)} %bitcast.40, f32[2,1536]{1,0:T(2,128)S(1)} %fusion.24), kind=kLoop, calls=%fused_computation.11 | loop fusion | flops 11010048 | bytes 9451520 | tf_op jit(solution)/shard_map/convert_element_type | solution.py:102
  97.9 1.9 convolution_convert_fusion.1
  99.9 1.9 convolution_convert_fusion
  101.8 3.5 %pad_maximum_fusion = bf16[16,64,3072]{2,1,0:T(8,128)(2,1)} fusion(bf16[16,64,1536]{2,1,0:T(8,128)(2,1)S(1)} %bitcast.38, bf16[16,64,1536]{2,1,0:T(8,128)(2,1)S(1)} %bitcast.37), kind=kLoop, calls=%fused_computation.1 | loop fusion | flops 12582912 | bytes 12582912 | tf_op jit(solution)/shard_map/concatenate | solution.py:105
  105.3 9.4 %all-to-all-start = ((bf16[16,64,3072]{2,1,0:T(8,128)(2,1)}), bf16[16,64,3072]{2,1,0:T(8,128)(2,1)}, u32[]{:S(2)}, u32[]{:S(2)}) async-start(bf16[16,64,3072]{2,1,0:T(8,128)(2,1)} %pad_maximum_fusion), calls=%async_computation.1 | async-start | bytes 12582912 | tf_op jit(solution)/shard_map/all_to_all | solution.py:107
  114.7 1.2 fusion.13
  115.9 136.2 %all-to-all-done = bf16[16,64,3072]{2,1,0:T(8,128)(2,1)} async-done(((bf16[16,64,3072]{2,1,0:T(8,128)(2,1)}), bf16[16,64,3072]{2,1,0:T(8,128)(2,1)}, u32[]{:S(2)}, u32[]{:S(2)}) %all-to-all-start) | async-done | bytes 6291488 | tf_op jit(solution)/shard_map/all_to_all | solution.py:107
  252.1 4.0 %convert_reduce_fusion = f32[64,3072]{1,0:T(8,128)S(1)} fusion(bf16[16,64,3072]{2,1,0:T(8,128)(2,1)} %all-to-all-done), kind=kLoop, calls=%fused_computation | loop fusion | flops 6094848 | bytes 7077888 | tf_op jit(solution)/shard_map/reduce_sum | solution.py:108
  256.1 0.9 fusion.34
  (38 shorter events, 0.3 us)
Async XLA Ops:
  7.2 10.5 %copy-start = (bf16[1024,1536]{1,0:T(8,128)(2,1)S(1)}, bf16[1024,1536]{1,0:T(8,128)(2,1)}, u32[]{:S(2)}) copy-start(bf16[1024,1536]{1,0:T(8,128)(2,1)} %param.14) | copy-start | bytes 9437188
  7.2 3.1 %copy-start.13 = (s32[2]{0:T(128)S(1)}, s32[2]{0:T(128)}, u32[]{:S(2)}) copy-start(s32[2]{0:T(128)} %param.11) | copy-start | bytes 28
  7.2 4.7 %copy-start.12 = (bf16[1024]{0:T(1024)(128)(2,1)S(1)}, bf16[1024]{0:T(1024)(128)(2,1)}, u32[]{:S(2)}) copy-start(bf16[1024]{0:T(1024)(128)(2,1)} %param.12) | copy-start | bytes 6148
  7.2 59.0 %reduce-scatter.2.cloned.1.call-start = ((), (), s32[]{:S(2)}) async-start(), calls=%async_computation.2 | async-start | bytes 557056 | tf_op jit(solution)/shard_map/reduce_scatter | solution.py:40
  11.9 5.8 %copy-start.8 = (f32[512]{0:T(512)}, f32[512]{0:T(512)S(1)}, u32[]{:S(2)}) copy-start(f32[512]{0:T(512)S(1)} %add_rsqrt_fusion) | copy-start | bytes 6148
  11.9 5.7 %copy-start.6 = (f32[1024]{0:T(1024)}, f32[1024]{0:T(1024)S(1)}, u32[]{:S(2)}) copy-start(f32[1024]{0:T(1024)S(1)} %convert_element_type.57) | copy-start | bytes 12292
  13.5 4.2 %copy-start.3 = (bf16[512,1024]{1,0:T(8,128)(2,1)S(1)}, bf16[512,1024]{1,0:T(8,128)(2,1)}, u32[]{:S(2)}) copy-start(bf16[512,1024]{1,0:T(8,128)(2,1)} %param.10) | copy-start | bytes 3145732
  17.7 3.9 %copy-start.1 = (f32[512,1536]{1,0:T(8,128)}, f32[512,1536]{1,0:T(8,128)S(1)}, u32[]{:S(2)}) copy-start(f32[512,1536]{1,0:T(8,128)S(1)} %fusion.33) | copy-start | bytes 9437188
  41.5 0.8 copy-start.5
  42.4 0.6 copy-start.11
  85.9 8.4 %copy-start.10 = (f32[1,2,2,128]{3,1,2,0:T(2,128)S(1)}, f32[1,2,2,128]{3,1,2,0:T(2,128)}, u32[]{:S(2)}) copy-start(f32[1,2,2,128]{3,1,2,0:T(2,128)} %copy.14) | copy-start | bytes 6148
  89.5 4.8 %copy-start.2 = (f32[512,1536]{1,0:T(8,128)S(1)}, f32[512,1536]{1,0:T(8,128)}, u32[]{:S(2)}) copy-start(f32[512,1536]{1,0:T(8,128)} %copy-done.1) | copy-start | bytes 9437188
  94.3 3.6 %copy-start.4 = (bf16[512,1024]{1,0:T(8,128)(2,1)S(1)}, bf16[512,1024]{1,0:T(8,128)(2,1)}, u32[]{:S(2)}) copy-start(bf16[512,1024]{1,0:T(8,128)(2,1)} %param.10) | copy-start | bytes 3145732
  94.4 3.6 %copy-start.7 = (f32[1024]{0:T(1024)S(1)}, f32[1024]{0:T(1024)}, u32[]{:S(2)}) copy-start(f32[1024]{0:T(1024)} %copy-done.6) | copy-start | bytes 12292
  94.4 3.6 %copy-start.9 = (f32[512]{0:T(512)S(1)}, f32[512]{0:T(512)}, u32[]{:S(2)}) copy-start(f32[512]{0:T(512)} %copy-done.8) | copy-start | bytes 6148
  105.3 9.4 %slice-start = ((f32[32,2688]{1,0:T(8,128)}), f32[32,1536]{1,0:T(8,128)S(1)}, s32[]{:S(2)}) async-start(f32[32,2688]{1,0:T(8,128)} %copy-done.5), calls=%async_computation.3 | async-start | bytes 393216 | tf_op jit(solution)/shard_map/slice | solution.py:65
  105.3 146.8 %all-to-all-start = ((bf16[16,64,3072]{2,1,0:T(8,128)(2,1)}), bf16[16,64,3072]{2,1,0:T(8,128)(2,1)}, u32[]{:S(2)}, u32[]{:S(2)}) async-start(bf16[16,64,3072]{2,1,0:T(8,128)(2,1)} %pad_maximum_fusion), calls=%async_computation.1 | async-start | bytes 12582912 | tf_op jit(solution)/shard_map/all_to_all | solution.py:107
Sparse Core Ops, SparseCore 0:
  11.6 54.5 reduce-scatter.1
